TPU v7x, 32 devices: a whole 2x2x4 slice. The times are simulated.
32 devices in a mesh: ctx: 4 (over x, core), tp: 8 (over z, y).
Axes of the slice: x: 2, y: 2, z: 4, core: 2. Of those that a mesh axis runs over, the one named last changes fastest.
Arguments:
- token_ids: int32 [1024], replicated, may hold values from 0 to 128255
- doc_lengths: int32 [8], replicated, may hold values from 1 to 256, 1024 in all
- block_order: int32 [8], replicated, may hold values from 0 to 7, each once
- table: bfloat16 [128256, 8192], P('tp', 'ctx'), may hold values from -6 to 6
- gain: float32 [8192], replicated, may hold values from 0.5 to 12, as said below
- w_query: bfloat16 [8192, 8192], P('ctx', 'tp'), may hold values from -0.0625 to 0.0625
- w_keyval: bfloat16 [8192, 2, 1024], P('ctx'), may hold values from -0.0625 to 0.0625
Outputs:
- attended: bfloat16 [1024, 8192], P('ctx', 'tp')
Inputs may be any that keep to these rules, and one draw needn't show every extreme that they name: `token_ids`: ids of the vocabulary. `doc_lengths`: the documents fill the slab in order, their lengths sum to 1024. `block_order`: a permutation of the 8 blocks of the slab. `gain`: positive gains.
All inputs are finite; a program needn't handle non-finite values.
Results may differ from a plain program's by a relative error of at most 0.007.
The roundings to bfloat16 on the way count: a program that leaves them out, or rounds other values in their place, can miss the bound.
Values may be sent and summed in bfloat16 or wider, within the bound.
A program may use at most 128 MiB of HBM per device.

v0:
```python
import jax
import jax.numpy as jnp
from jax import lax
from jax.sharding import PartitionSpec as P

HEADS = 64
KV_HEADS = 8
HD = 128
BLOCK = 128
rotary_base = 500000.0


def rotary(values_in, pos_rows):
    half_dim = values_in.shape[-1] // 2
    steps_up = jnp.arange(half_dim, dtype=jnp.float32)
    freqs = jnp.power(rotary_base, -2.0 * steps_up / values_in.shape[-1])
    angle = pos_rows.astype(jnp.float32)[:, None] * freqs[None, :]
    angle = angle.reshape((angle.shape[0],) + (1,) * (values_in.ndim - 2) + (half_dim,))
    cosine = jnp.cos(angle)
    sine = jnp.sin(angle)
    first = values_in[..., :half_dim]
    second = values_in[..., half_dim:]
    return jnp.concatenate(
        [first * cosine - second * sine, second * cosine + first * sine], axis=-1
    )


def document_of(pos_rows, doc_lengths):
    ends = jnp.cumsum(doc_lengths)
    return jnp.sum((ends[None, :] <= pos_rows[:, None]).astype(jnp.int32), axis=1)


def shards(token_ids, doc_lengths, block_order, table, gain, w_query, w_keyval):
    ctx_count = lax.axis_size("ctx")
    ctx_at = lax.axis_index("ctx")
    tp_count = lax.axis_size("tp")
    tp_at = lax.axis_index("tp")
    tokens_all = token_ids.shape[0]
    tok_here = tokens_all // ctx_count
    vocab_here = table.shape[0]
    columns = table.shape[1]
    width = gain.shape[0]
    heads_here = HEADS // tp_count
    row_index = jnp.arange(tokens_all, dtype=jnp.int32)
    positions = block_order[row_index // BLOCK] * BLOCK + row_index % BLOCK
    local_ids = token_ids[positions] - tp_at * vocab_here
    inside = (local_ids >= 0) & (local_ids < vocab_here)
    picked = jnp.take(table, jnp.clip(local_ids, 0, vocab_here - 1), axis=0)
    partial_value = jnp.where(inside[:, None], picked, jnp.zeros_like(picked))
    kv_head = tp_at * heads_here // (HEADS // KV_HEADS)
    w_pair = lax.dynamic_slice_in_dim(w_keyval, kv_head * HD, HD, 2).reshape(
        w_keyval.shape[0], 2 * HD
    )
    col_embed = lax.psum(partial_value, "tp").astype(jnp.float32)
    gain_here = lax.dynamic_slice_in_dim(gain, ctx_at * columns, columns)
    col_scaled = (col_embed * gain_here).astype(jnp.bfloat16)
    query_term = jnp.dot(col_scaled, w_query, preferred_element_type=jnp.float32)
    pair_term = jnp.dot(col_scaled, w_pair, preferred_element_type=jnp.float32)
    square_term = jnp.sum(col_embed * col_embed, axis=1)
    query_raw, pair_raw, sumsq = (
        lax.psum_scatter(query_term, "ctx", scatter_dimension=0, tiled=True),
        lax.psum_scatter(pair_term, "ctx", scatter_dimension=0, tiled=True),
        lax.psum_scatter(square_term, "ctx", scatter_dimension=0, tiled=True),
    )
    inverse = lax.rsqrt(sumsq / width + 1e-05)
    my_pos = lax.dynamic_slice_in_dim(positions, ctx_at * tok_here, tok_here)
    query_rows = rotary(
        (query_raw * inverse[:, None]).reshape(tok_here, heads_here, HD), my_pos
    ).astype(jnp.bfloat16)
    key_rows = rotary(pair_raw[:, :HD] * inverse[:, None], my_pos).astype(jnp.bfloat16)
    value_rows = (pair_raw[:, HD:] * inverse[:, None]).astype(jnp.bfloat16)
    my_doc = document_of(my_pos, doc_lengths)
    stacked = jnp.transpose(query_rows, (1, 0, 2)).reshape(heads_here * tok_here, HD)
    query_pos = jnp.tile(my_pos, heads_here)
    query_doc = jnp.tile(my_doc, heads_here)
    inv_root = 1.0 / jnp.sqrt(jnp.float32(HD))
    query_total = heads_here * tok_here
    key_piece = lax.all_gather(key_rows, "ctx", axis=0, tiled=True)
    value_piece = lax.all_gather(value_rows, "ctx", axis=0, tiled=True)
    key_doc = document_of(positions, doc_lengths)
    allowed = (key_doc[None, :] == query_doc[:, None]) & (positions[None, :] <= query_pos[:, None])
    largest = jnp.full((query_total,), -1e30, jnp.float32)
    scores = (
        lax.dot_general(
            stacked, key_piece, (((1,), (1,)), ((), ())), preferred_element_type=jnp.float32
        )
        * inv_root
    )
    masked = jnp.where(allowed, scores, jnp.float32(-1e30))
    new_largest = jnp.maximum(largest, jnp.max(masked, axis=1))
    weights = jnp.where(allowed, jnp.exp(masked - new_largest[:, None]), jnp.float32(0.0))
    new_totals = jnp.sum(weights, axis=1)
    new_accum = jnp.dot(
        weights.astype(jnp.bfloat16), value_piece, preferred_element_type=jnp.float32
    )
    mixed = (new_accum / new_totals[:, None]).reshape(heads_here, tok_here, HD)
    return jnp.transpose(mixed, (1, 0, 2)).reshape(tok_here, heads_here * HD).astype(jnp.bfloat16)


def solution(mesh):
    in_specs = (P(), P(), P(), P("tp", "ctx"), P(), P("ctx", "tp"), P("ctx", None, None))
    out_specs = P("ctx", "tp")
    return jax.shard_map(shards, mesh=mesh, in_specs=in_specs, out_specs=out_specs, check_vma=False)
```

profile of v0, /device:TPU:0, one launch (start us, length us, event | category | flops | bytes accessed | tf_op | source)
XLA Modules:
  0.0 328.4 jit_solution(2111878941764237552)
XLA Ops:
  6.5 0.0 copy-start
  6.5 0.0 all-reduce.3.cloned.1.call-start
  6.6 1.6 fusion.32
  8.2 4.3 %compare_select_fusion.3 = s32[1024,1]{0,1:T(1,128)S(1)} fusion(s32[]{:T(128)} %bitcast.3, s32[]{:T(128)} %bitcast.4, s32[]{:T(128)} %bitcast.5, s32[]{:T(128)} %bitcast.6, s32[]{:T(128)} %bitcast.7, s32[]{:T(128)} %bitcast.9, s32[]{:T(128)} %bitcast.8), kind=kLoop, calls=%fused_computation.38 | loop fusion | flops 23552 | bytes 4124 | tf_op jit(solution)/shard_map/gather | solution.py:45
  12.5 0.7 fusion.21
  13.2 0.0 copy-done
  13.2 4.5 %gather_fusion = s32[1024]{0:T(1024)S(1)} fusion(s32[1024]{0:T(1024)S(1)} %copy-done, s32[1024]{0:T(1024)S(1)} %broadcast_clamp_fusion.1), kind=kCustom, calls=%fused_computation | custom fusion | bytes 12288 | tf_op jit(solution)/shard_map/gather | solution.py:46
  17.8 52.7 %gather_fusion.1 = bf16[1024,2048]{1,0:T(8,128)(2,1)} fusion(bf16[16032,2048]{1,0:T(8,128)(2,1)} %param.10, s32[1024]{0:T(1024)S(1)} %broadcast_clamp_fusion), kind=kCustom, calls=%fused_computation.1 | custom fusion | bytes 8392704 | tf_op jit(solution)/shard_map/jit(_take)/gather | solution.py:48
  70.5 4.1 %select_select_fusion = bf16[1024,2048]{1,0:T(8,128)(2,1)} fusion(bf16[1024,2048]{1,0:T(8,128)(2,1)} %gather_fusion.1, pred[1024]{0:T(1024)(128)(4,1)S(1)} %get-tuple-element.9, pred[1024]{0:T(1024)(128)(4,1)S(1)} %get-tuple-element.19), kind=kLoop, calls=%fused_computation.12 | loop fusion | flops 4194304 | bytes 8390656 | tf_op jit(solution)/shard_map/jit(_where)/select_n | solution.py:49
  74.6 0.0 all-reduce.3.cloned.1.call-update
  74.6 0.0 reduce-scatter.5.cloned.1.call-start
  74.7 0.7 dynamic_slice.10
  75.4 1.8 constant_dynamic-slice_fusion
  77.2 156.5 %all-reduce.3.cloned.1.call-done = bf16[1024,2048]{1,0:T(8,128)(2,1)} async-done(((bf16[1024,2048]{1,0:T(8,128)(2,1)}), bf16[1024,2048]{1,0:T(8,128)(2,1)}) %all-reduce.3.cloned.1.call-update) | async-done | bytes 4194320 | tf_op jit(solution)/shard_map/psum | solution.py:54
  233.7 4.4 %fusion.7 = f32[1024,256]{1,0:T(8,128)} fusion(bf16[1024,2048]{1,0:T(8,128)(2,1)} %all-reduce.3.cloned.1.call-done, f32[2048]{0:T(1024)S(1)} %dynamic_slice.10, bf16[256,8,2,128]{3,2,1,0:T(2,128)(2,1)S(1)} %bitcast.44), kind=kOutput, calls=%fused_computation.14 | convolution fusion | flops 1080033280 | bytes 6299648 | tf_op jit(solution)/shard_map/dot_general | solution.py:58
  238.1 0.0 reduce-scatter.5.cloned.1.call-update
  238.1 0.0 copy-start.2
  238.1 0.0 copy-start.3
  238.1 0.0 reduce-scatter.3.cloned.1.call-start
  238.2 9.9 %fusion.9 = f32[1024,1024]{1,0:T(8,128)} fusion(bf16[2048,1024]{1,0:T(8,128)(2,1)} %param.12, bf16[1024,2048]{1,0:T(8,128)(2,1)} %all-reduce.3.cloned.1.call-done, f32[2048]{0:T(1024)S(1)} %dynamic_slice.10), kind=kOutput, calls=%fused_computation.15 | convolution fusion | flops 4301258752 | bytes 12591104 | tf_op jit(solution)/shard_map/dot_general | solution.py:57
  248.1 0.0 reduce-scatter.3.cloned.1.call-update
  248.1 0.0 copy-done.2
  248.2 0.2 reduce-window.8
  248.3 0.1 fusion.30
  248.4 0.1 convert_reduce_fusion.1
  248.5 0.0 copy-done.3
  248.5 0.6 dynamic-slice
  249.8 0.1 convert_reduce_fusion
  249.9 3.1 fusion.1
  253.0 7.3 %all-reduce = f32[1024]{0:T(1024)S(1)} all-reduce(f32[1024]{0:T(1024)S(1)} %fusion.1), channel_id=3, replica_groups=mesh['ctx'=4,'tp'=8] {'ctx'}, use_global_device_ids=true, to_apply=%region_6.7.clone | all-reduce | flops 1024 | bytes 8192
  260.2 0.1 fusion.26
  260.3 1.9 reduce-scatter.5.cloned.1.call-done
  262.2 1.1 slice_multiply_fusion.1
  263.2 0.6 subtract_convert_fusion.1
  263.8 0.1 pad_maximum_fusion.1
  263.9 5.8 %all_gather.6 = bf16[1024,128]{1,0:T(8,128)(2,1)S(1)} all-gather(bf16[256,128]{1,0:T(8,128)(2,1)S(1)} %pad_maximum_fusion.1), channel_id=1, replica_groups=mesh['ctx'=4,'tp'=8] {'ctx'}, dimensions={0}, use_global_device_ids=true | all-gather | bytes 327680 | tf_op jit(solution)/shard_map/all_gather | solution.py:78
  269.7 6.0 %all_gather.7 = bf16[1024,128]{1,0:T(8,128)(2,1)S(1)} all-gather(bf16[256,128]{1,0:T(8,128)(2,1)S(1)} %get-tuple-element.16), channel_id=1, replica_groups=mesh['ctx'=4,'tp'=8] {'ctx'}, dimensions={0}, use_global_device_ids=true | all-gather | bytes 327680 | tf_op jit(solution)/shard_map/all_gather | solution.py:79
  275.7 33.6 %reduce-scatter.3.cloned.1.call-done = f32[256,1024]{1,0:T(8,128)} async-done(((f32[1024,1024]{1,0:T(8,128)}), f32[256,1024]{1,0:T(8,128)}) %reduce-scatter.3.cloned.1.call-update) | async-done | bytes 1048592 | tf_op jit(solution)/shard_map/reduce_scatter | solution.py:61
  309.3 1.4 multiply_bitcast_fusion
  310.7 0.2 copy.23
  310.9 0.3 fusion.31
  311.2 0.4 subtract_convert_fusion
  311.6 0.3 pad_maximum_fusion
  311.9 2.1 fusion.2
  314.1 0.0 copy-start.1
  314.1 3.8 %fusion.3 = f32[2048]{0:T(1024)S(1)} fusion(f32[2048,1024]{0,1:T(8,128)S(1)} %get-tuple-element.31, f32[2048]{0:T(1024)S(1)} %broadcast_maximum_fusion, s32[2048]{0:T(1024)S(1)} %bitcast.51, s32[2048]{0:T(1024)S(1)} %bitcast.48, s32[1024]{0:T(1024)S(1)} %get-tuple-element.7, s32[1024]{0:T(1024)S(1)} %convert_reduce_fusion), kind=kLoop, calls=%fused_computation.10 | loop fusion | flops 16775168 | bytes 8429568 | tf_op jit(solution)/shard_map/reduce_sum | solution.py:92
  317.9 3.1 fusion.14
  320.9 0.9 copy.34
  (13 shorter events, 0.1 us)
Async XLA Ops:
  6.5 6.6 %copy-start = (s32[1024]{0:T(1024)S(1)}, s32[1024]{0:T(1024)}, u32[]{:S(2)}) copy-start(s32[1024]{0:T(1024)} %param.7) | copy-start | bytes 12292
  6.5 227.1 %all-reduce.3.cloned.1.call-start = ((), (), s32[]{:S(2)}) async-start(), calls=%async_computation.2 | async-start | bytes 8388608 | tf_op jit(solution)/shard_map/psum | solution.py:54
  74.6 187.6 %reduce-scatter.5.cloned.1.call-start = ((), (), s32[]{:S(2)}) async-start(), calls=%async_computation.4 | async-start | bytes 1310720 | tf_op jit(solution)/shard_map/reduce_scatter | solution.py:62
  238.1 10.0 %copy-start.2 = (s32[8]{0:T(128)S(1)}, s32[8]{0:T(128)}, u32[]{:S(2)}) copy-start(s32[8]{0:T(128)} %param.8) | copy-start | bytes 100
  238.1 10.4 %copy-start.3 = (u32[32]{0:T(128)S(1)}, u32[32]{0:T(128)}, u32[]{:S(2)}) copy-start(u32[32]{0:T(128)} %constant.126) | copy-start | bytes 388
  238.1 71.2 %reduce-scatter.3.cloned.1.call-start = ((), (), s32[]{:S(2)}) async-start(), calls=%async_computation.3 | async-start | bytes 5242880 | tf_op jit(solution)/shard_map/reduce_scatter | solution.py:61
  314.1 7.8 %copy-start.1 = (s32[1024]{0:T(1024)S(1)}, s32[1024]{0:T(1024)}, u32[]{:S(2)}) copy-start(s32[1024]{0:T(1024)} %param.7) | copy-start | bytes 12292
Sparse Core Ops, SparseCore 0:
  74.7 158.8 all-reduce.2
  238.2 23.8 reduce-scatter.4
  264.7 44.5 reduce-scatter.2
where the time goes:
time: 330 us; the launch traced here: 328 us
  waiting for transfers between devices  192 us (58%)
  local copies, waits for them, and re-layouts  63.5 us (19%)
  other arithmetic  20.2 us (6%)
  matrix products  19.5 us (6%)
  blocking collectives  19.1 us (6%)
  between operations  14 us (4%)
    psum x1, waiting for transfers between devices, shards(): col_embed = lax.psum(partial_value, 'tp').astype(jnp.float32)  156 us
    gather x1, local copies, waits for them, and re-layouts, shards(): picked = jnp.take(table, jnp.clip(local_ids, 0, vocab_here - 1), axis=0)  52.7 us
    reduce_scatter x1, waiting for transfers between devices, shards(): lax.psum_scatter(query_term, 'ctx', scatter_dimension=0, tiled=True)  33.6 us
    dot_general x1, matrix products, shards(): jnp.dot(col_scaled, w_query, preferred_element_type=jnp.float32)  9.92 us
    unnamed x1, blocking collectives  7.27 us
  transfers between devices with their start and end apart: 3, of which 3 were waited for; matrix products, arithmetic and copies ran while one was open for 6% of the time, Pallas kernels for 0%

commit v1 on v0

--- a/solution.py
+++ b/solution.py
@@ -51,7 +51,7 @@
     w_pair = lax.dynamic_slice_in_dim(w_keyval, kv_head * HD, HD, 2).reshape(
         w_keyval.shape[0], 2 * HD
     )
-    col_embed = lax.psum(partial_value, "tp").astype(jnp.float32)
+    col_embed = jnp.sum(lax.all_gather(partial_value, "tp"), axis=0).astype(jnp.float32)
     gain_here = lax.dynamic_slice_in_dim(gain, ctx_at * columns, columns)
     col_scaled = (col_embed * gain_here).astype(jnp.bfloat16)
     query_term = jnp.dot(col_scaled, w_query, preferred_element_type=jnp.float32)

time: 330 us -> 826 us (2.50)
  waiting for transfers between devices: 192 us -> 674 us
  other arithmetic: 20.2 us -> 34.6 us
    all_gather x0 -> x1, waiting for transfers between devices: none -> 638 us  [shards(): lax.all_gather(partial_value, 'tp')]
    psum x1 -> x0, waiting for transfers between devices: 156 us -> none  [shards(): col_embed = lax.psum(partial_value, 'tp').astype(jnp.float32)]
    reduce_sum x0 -> x1, other arithmetic: none -> 14.2 us  [shards(): jnp.sum(lax.all_gather(partial_value, 'tp'), axis=0).astype(jnp.float32)]
  transfers between devices with their start and end apart: 3 -> 3, of which waited for: 3 -> 3; matrix products, arithmetic and copies ran while one was open for 6% -> 2% of each run, Pallas kernels for 0% -> 0%
where the time goes in v1:
time: 826 us; the launch traced here: 825 us
  waiting for transfers between devices  674 us (82%)
  local copies, waits for them, and re-layouts  63.4 us (8%)
  other arithmetic  34.6 us (4%)
  matrix products  19.6 us (2%)
  blocking collectives  19.1 us (2%)
  between operations  14 us (2%)
    all_gather x1, waiting for transfers between devices, shards(): lax.all_gather(partial_value, 'tp')  638 us
    gather x1, local copies, waits for them, and re-layouts, shards(): picked = jnp.take(table, jnp.clip(local_ids, 0, vocab_here - 1), axis=0)  52.7 us
    reduce_scatter x1, waiting for transfers between devices, shards(): lax.psum_scatter(query_term, 'ctx', scatter_dimension=0, tiled=True)  33.6 us
  transfers between devices with their start and end apart: 3, of which 3 were waited for; matrix products, arithmetic and copies ran while one was open for 2% of the time, Pallas kernels for 0%

profile of v1, /device:TPU:0, one launch (start us, length us, event | category | flops | bytes accessed | tf_op | source)
XLA Modules:
  0.0 825.0 jit_solution(1896347978864197796)
XLA Ops:
  6.5 0.0 copy-start
  6.5 0.0 all-gather.2.cloned.1.call-start
  6.6 1.6 fusion.33
  8.2 4.3 compare_select_fusion.3
  12.5 0.7 fusion.22
  13.2 0.0 copy-done
  13.2 4.5 gather_fusion
  17.8 52.7 %gather_fusion.1 = bf16[1024,2048]{1,0:T(8,128)(2,1)} fusion(bf16[16032,2048]{1,0:T(8,128)(2,1)} %param.10, s32[1024]{0:T(1024)S(1)} %broadcast_clamp_fusion), kind=kCustom, calls=%fused_computation.1 | custom fusion | bytes 8392704 | tf_op jit(solution)/shard_map/jit(_take)/gather | solution.py:48
  70.5 4.1 fusion.5
  74.6 0.0 all-gather.2.cloned.1.call-update
  74.6 0.0 reduce-scatter.5.cloned.1.call-start
  74.7 0.7 dynamic_slice.10
  75.4 1.8 constant_dynamic-slice_fusion
  77.2 637.7 %all-gather.2.cloned.1.call-done = bf16[8,1024,2048]{2,1,0:T(8,128)(2,1)} async-done(((bf16[1,1024,2048]{2,1,0:T(8,128)(2,1)}), bf16[8,1024,2048]{2,1,0:T(8,128)(2,1)}) %all-gather.2.cloned.1.call-update) | async-done | bytes 33554448 | tf_op jit(solution)/shard_map/all_gather | solution.py:54
  715.0 14.2 %reduce_sum.50 = bf16[1024,2048]{1,0:T(8,128)(2,1)} reduce(bf16[8,1024,2048]{2,1,0:T(8,128)(2,1)} %all-gather.2.cloned.1.call-done, bf16[]{:T(256)} %constant.105.clone.1), dimensions={0}, to_apply=%region_3.4 | reduce | flops 14680064 | bytes 37748736 | tf_op jit(solution)/shard_map/reduce_sum | solution.py:54
  729.2 4.5 fusion.8
  733.7 0.0 reduce-scatter.5.cloned.1.call-update
  733.7 0.0 copy-start.2
  733.7 0.0 copy-start.3
  733.7 0.0 reduce-scatter.3.cloned.1.call-start
  733.8 9.9 %fusion.10 = f32[1024,1024]{1,0:T(8,128)} fusion(bf16[2048,1024]{1,0:T(8,128)(2,1)} %param.12, bf16[1024,2048]{1,0:T(8,128)(2,1)} %reduce_sum.50, f32[2048]{0:T(1024)S(1)} %dynamic_slice.10), kind=kOutput, calls=%fused_computation.16 | convolution fusion | flops 4301258752 | bytes 12591104 | tf_op jit(solution)/shard_map/dot_general | solution.py:57
  743.7 0.0 reduce-scatter.3.cloned.1.call-update
  743.7 0.2 reduce-window.8
  743.9 0.1 fusion.31
  744.0 0.1 convert_reduce_fusion.1
  744.1 0.0 copy-done.3
  744.1 0.6 dynamic-slice
  745.3 0.1 convert_reduce_fusion
  745.4 3.1 fusion.1
  748.5 7.3 all-reduce
  755.8 0.1 fusion.27
  755.9 2.9 reduce-scatter.5.cloned.1.call-done
  758.8 1.1 slice_multiply_fusion.1
  759.8 0.6 subtract_convert_fusion.1
  760.4 0.1 pad_maximum_fusion.1
  760.5 5.8 all_gather.11
  766.3 6.0 all_gather.12
  772.3 33.6 %reduce-scatter.3.cloned.1.call-done = f32[256,1024]{1,0:T(8,128)} async-done(((f32[1024,1024]{1,0:T(8,128)}), f32[256,1024]{1,0:T(8,128)}) %reduce-scatter.3.cloned.1.call-update) | async-done | bytes 1048592 | tf_op jit(solution)/shard_map/reduce_scatter | solution.py:61
  805.9 1.4 multiply_bitcast_fusion
  807.2 0.2 copy.23
  807.4 0.3 fusion.32
  807.8 0.4 subtract_convert_fusion
  808.2 0.3 pad_maximum_fusion
  808.5 2.1 fusion.2
  810.6 0.0 copy-start.1
  810.7 3.8 fusion.3
  814.4 3.1 fusion.15
  817.5 0.9 copy.34
  (14 shorter events, 0.1 us)
Async XLA Ops:
  6.5 6.6 copy-start
  6.5 708.4 %all-gather.2.cloned.1.call-start = ((), (), s32[]{:S(2)}) async-start(), calls=%async_computation.2 | async-start | bytes 37748736 | tf_op jit(solution)/shard_map/all_gather | solution.py:54
  74.6 684.1 %reduce-scatter.5.cloned.1.call-start = ((), (), s32[]{:S(2)}) async-start(), calls=%async_computation.4 | async-start | bytes 1310720 | tf_op jit(solution)/shard_map/reduce_scatter | solution.py:62
  733.7 10.0 %copy-start.2 = (s32[8]{0:T(128)S(1)}, s32[8]{0:T(128)}, u32[]{:S(2)}) copy-start(s32[8]{0:T(128)} %param.8) | copy-start | bytes 100
  733.7 10.4 %copy-start.3 = (u32[32]{0:T(128)S(1)}, u32[32]{0:T(128)}, u32[]{:S(2)}) copy-start(u32[32]{0:T(128)} %constant.127) | copy-start | bytes 388
  733.7 72.1 %reduce-scatter.3.cloned.1.call-start = ((), (), s32[]{:S(2)}) async-start(), calls=%async_computation.3 | async-start | bytes 5242880 | tf_op jit(solution)/shard_map/reduce_scatter | solution.py:61
  810.6 7.8 copy-start.1
Sparse Core Ops, SparseCore 0:
  74.8 640.1 all-gather.1
  733.8 24.8 reduce-scatter.4
  761.3 44.5 reduce-scatter.2
